TPU v7x, 32 devices: a whole 2x2x4 slice. The times are simulated.
32 devices in a mesh: tau: 2 (over y), aux: 16 (over z, x, core).
Axes of the slice: x: 2, y: 2, z: 4, core: 2. Of those that a mesh axis runs over, the one named last changes fastest.
Arguments:
- coefficients: bfloat16 [16384, 2048], P('aux'), may hold values from -0.125 to 0.125
- green_occ: bfloat16 [16, 2048, 2048], P('tau', 'aux'), may hold values from -6 to 6
- green_vir: bfloat16 [16, 2048, 2048], P('tau', 'aux'), may hold values from -6 to 6
- minimax: float32 [16, 16], replicated, may hold values from -1.5 to 1.5
- coulomb: float32 [512], replicated, may hold values from 0.006 to 0.04
Outputs:
- screened: float32 [16, 16384, 512], P('tau', 'aux')
All inputs are finite; a program needn't handle non-finite values.
Results may differ from a plain program's by a relative error of at most 0.0078.
Values may be sent and summed in bfloat16 or wider, within the bound.
No kernel may reach another device: no remote copies, remote signals or barrier semaphores. Data moves between devices by JAX's collectives and lax.ppermute only.
A program may use at most 128 MiB of HBM per device.

v0:
```python
import jax
import jax.numpy as jnp
from jax import lax
from jax.sharding import PartitionSpec as P

NAUX = 16384
PANEL = 512
DYSON = 4


def per_device(coefficients, green_occ, green_vir, minimax, coulomb):
    stride = NAUX // PANEL
    local_panel = coefficients[::stride]
    panel_coef = lax.all_gather(local_panel, "aux", axis=0, tiled=True)
    product = (green_occ.astype(jnp.float32) * green_vir.astype(jnp.float32)).astype(jnp.bfloat16)
    folded = jnp.einsum(
        "tkn,qn->tkq", product, panel_coef, preferred_element_type=jnp.float32
    ).astype(jnp.bfloat16)
    owners = lax.axis_size("tau")
    freq_count = minimax.shape[0] // owners
    own_rows = lax.dynamic_slice_in_dim(minimax, lax.axis_index("tau") * freq_count, freq_count, 0)
    gathered = lax.all_gather(folded, "tau", axis=0, tiled=True)
    mixed = jnp.einsum(
        "wt,tkq->wkq", own_rows, gathered.astype(jnp.float32), precision=lax.Precision.HIGHEST
    )
    wide_coef = coefficients.astype(jnp.float32)
    chi_freq = jnp.einsum(
        "pk,wkq->wpq",
        wide_coef,
        lax.all_gather(mixed, "aux", axis=1, tiled=True),
        precision=lax.Precision.HIGHEST,
    )
    coupling = lax.all_gather(chi_freq[:, ::stride, :], "aux", axis=1, tiled=True)
    screened = chi_freq
    for sweep in range(DYSON):
        screened = chi_freq + jnp.einsum(
            "wpq,wqr->wpr", screened * coulomb, coupling, precision=lax.Precision.HIGHEST
        )
    return screened


def solution(mesh):
    placed = (P("aux", None), P("tau", "aux", None), P("tau", "aux", None), P(), P())
    return jax.shard_map(
        per_device, mesh=mesh, in_specs=placed, out_specs=P("tau", "aux", None), check_vma=False
    )
```

profile of v0, /device:TPU:0, one launch (start us, length us, event | category | flops | bytes accessed | tf_op | source)
XLA Modules:
  0.0 695.1 jit_solution(247652757352555016)
XLA Ops:
  6.5 0.0 copy-start
  6.5 0.0 all-gather.5.cloned.1.call-start
  6.5 3.0 slice.6
  9.5 0.0 all-gather.5.cloned.1.call-update
  9.5 0.0 all-gather.7.cloned.1.call-start
  9.6 44.3 %all-gather.5.cloned.1.call-done = bf16[512,2048]{1,0:T(8,128)(2,1)} async-done(((bf16[32,2048]{1,0:T(8,128)(2,1)}), bf16[512,2048]{1,0:T(8,128)(2,1)}) %all-gather.5.cloned.1.call-update) | async-done | bytes 2097168 | tf_op jit(solution)/shard_map/all_gather | solution.py:14
  53.9 7.4 %fusion.27 = bf16[8,128,512]{2,1,0:T(8,128)(2,1)} fusion(bf16[512,2048]{1,0:T(8,128)(2,1)} %all-gather.5.cloned.1.call-done, bf16[8,128,2048]{2,1,0:T(8,128)(2,1)} %param.7, bf16[8,128,2048]{2,1,0:T(8,128)(2,1)} %param.6), kind=kOutput, calls=%fused_computation.27 | convolution fusion | flops 2156396544 | bytes 11534336 | tf_op jit(solution)/shard_map/tkn,qn->tkq/dot_general | solution.py:16
  61.3 0.0 all-gather.7.cloned.1.call-update
  61.3 0.0 all-gather.9.cloned.1.call-start
  61.3 31.9 %all-gather.7.cloned.1.call-done = bf16[16,128,512]{2,1,0:T(8,128)(2,1)} async-done(((bf16[8,128,512]{2,1,0:T(8,128)(2,1)}), bf16[16,128,512]{2,1,0:T(8,128)(2,1)}) %all-gather.7.cloned.1.call-update) | async-done | bytes 2097168 | tf_op jit(solution)/shard_map/all_gather | solution.py:22
  93.3 0.0 copy-done
  93.3 3.5 fusion.25
  96.7 1.9 copy.16
  98.6 0.0 all-gather.9.cloned.1.call-update
  98.6 0.0 copy-start.3
  98.7 0.3 all-gather.11.cloned.1.call-start
  98.9 175.6 %all-gather.9.cloned.1.call-done = f32[8,2048,512]{1,2,0:T(8,128)} async-done(((f32[8,128,512]{1,2,0:T(8,128)}), f32[8,2048,512]{1,2,0:T(8,128)}) %all-gather.9.cloned.1.call-update) | async-done | bytes 33554448 | tf_op jit(solution)/shard_map/all_gather | solution.py:30
  274.5 59.4 %convolution_bitcast_fusion = f32[8,1024,512]{1,2,0:T(8,128)} fusion(f32[8,2048,512]{1,2,0:T(8,128)} %all-gather.9.cloned.1.call-done, bf16[1024,2048]{1,0:T(8,128)(2,1)} %param.5), kind=kOutput, calls=%fused_computation.12 | convolution fusion | flops 103079215104 | bytes 54525952 | tf_op jit(solution)/shard_map/pk,wkq->wpq/dot_general | solution.py:27
  333.9 27.1 %slice.7 = f32[8,32,512]{1,2,0:T(8,128)S(1)} slice(f32[8,1024,512]{1,2,0:T(8,128)} %convolution_bitcast_fusion), slice={[0:8:1], [0:1024:32], [0:512:1]} | slice | bytes 1048576 | tf_op jit(solution)/shard_map/slice | solution.py:33
  361.1 1.4 copy.10
  362.5 0.0 all-gather.11.cloned.1.call-update
  362.5 72.2 %all-gather.11.cloned.1.call-done = f32[8,512,512]{2,0,1:T(8,128)} async-done(((f32[8,32,512]{2,0,1:T(8,128)}), f32[8,512,512]{2,0,1:T(8,128)}) %all-gather.11.cloned.1.call-update) | async-done | bytes 8388624 | tf_op jit(solution)/shard_map/all_gather | solution.py:33
  434.8 0.0 copy-done.3
  434.8 0.0 copy-start.2
  434.8 75.6 %fusion.9 = f32[8,1024,512]{1,2,0:T(8,128)} fusion(f32[8,1024,512]{1,2,0:T(8,128)} %convolution_bitcast_fusion, f32[512]{0:T(512)S(1)} %copy-done.3, f32[8,512,512]{2,0,1:T(8,128)} %all-gather.11.cloned.1.call-done), kind=kOutput, calls=%fused_computation.9 | convolution fusion | flops 25773998080 | bytes 41945088 | tf_op jit(solution)/shard_map/wpq,wqr->wpr/dot_general | solution.py:36
  510.4 0.0 copy-done.2
  510.4 41.5 %fusion.6 = f32[8,1024,512]{1,2,0:T(8,128)} fusion(f32[8,1024,512]{1,2,0:T(8,128)} %convolution_bitcast_fusion, f32[8,1024,512]{1,2,0:T(8,128)} %fusion.9, f32[512]{0:T(512)S(1)} %copy-done.3, f32[8,512,512]{2,0,1:T(8,128)S(1)} %copy-done.2), kind=kOutput, calls=%fused_computation.6 | convolution fusion | flops 25778192384 | bytes 58722304 | tf_op jit(solution)/shard_map/wpq,wqr->wpr/dot_general | solution.py:36
  551.9 41.5 %fusion.3 = f32[8,1024,512]{1,2,0:T(8,128)} fusion(f32[8,1024,512]{1,2,0:T(8,128)} %convolution_bitcast_fusion, f32[8,1024,512]{1,2,0:T(8,128)} %fusion.6, f32[512]{0:T(512)S(1)} %copy-done.3, f32[8,512,512]{2,0,1:T(8,128)S(1)} %copy-done.2), kind=kOutput, calls=%fused_computation.3 | convolution fusion | flops 25778192384 | bytes 58722304 | tf_op jit(solution)/shard_map/wpq,wqr->wpr/dot_general | solution.py:36
  593.3 78.4 %fusion.11 = f32[8,1024,512]{1,2,0:T(8,128)} fusion(f32[8,1024,512]{1,2,0:T(8,128)} %convolution_bitcast_fusion, f32[8,1024,512]{1,2,0:T(8,128)} %fusion.3, f32[512]{0:T(512)S(1)} %copy-done.3, f32[8,512,512]{2,0,1:T(8,128)} %all-gather.11.cloned.1.call-done), kind=kOutput, calls=%fused_computation.11 | convolution fusion | flops 25782386688 | bytes 58722304 | tf_op jit(solution)/shard_map/wpq,wqr->wpr/dot_general | solution.py:36
  671.7 0.0 copy-start.1
  671.7 16.4 %copy.14 = f32[8,1024,512]{2,1,0:T(8,128)} copy(f32[8,1024,512]{1,2,0:T(8,128)} %fusion.11) | data formatting | bytes 33554432 | tf_op jit(solution)/shard_map/add | solution.py:36
  688.2 0.0 copy-done.1
Async XLA Ops:
  6.5 86.7 %copy-start = (f32[16,16]{1,0:T(8,128)S(1)}, f32[16,16]{1,0:T(8,128)}, u32[]{:S(2)}) copy-start(f32[16,16]{1,0:T(8,128)} %param.8) | copy-start | bytes 3076
  6.5 47.3 %all-gather.5.cloned.1.call-start = ((), (), s32[]{:S(2)}) async-start(), calls=%async_computation | async-start | bytes 2228224 | tf_op jit(solution)/shard_map/all_gather | solution.py:14
  9.5 83.7 %all-gather.7.cloned.1.call-start = ((), (), s32[]{:S(2)}) async-start(), calls=%async_computation.1 | async-start | bytes 3145728 | tf_op jit(solution)/shard_map/all_gather | solution.py:22
  61.3 213.2 %all-gather.9.cloned.1.call-start = ((), (), s32[]{:S(2)}) async-start(), calls=%async_computation.2 | async-start | bytes 35651584 | tf_op jit(solution)/shard_map/all_gather | solution.py:30
  98.6 336.1 %copy-start.3 = (f32[512]{0:T(512)S(1)}, f32[512]{0:T(512)}, u32[]{:S(2)}) copy-start(f32[512]{0:T(512)} %param.9) | copy-start | bytes 6148
  98.7 336.1 %all-gather.11.cloned.1.call-start = ((), (), s32[]{:S(2)}) async-start(), calls=%async_computation.3 | async-start | bytes 8912896 | tf_op jit(solution)/shard_map/all_gather | solution.py:33
  434.8 75.6 %copy-start.2 = (f32[8,512,512]{2,0,1:T(8,128)S(1)}, f32[8,512,512]{2,0,1:T(8,128)}, u32[]{:S(2)}) copy-start(f32[8,512,512]{2,0,1:T(8,128)} %all-gather.11.cloned.1.call-done) | copy-start | bytes 25165828
  671.7 16.4 %copy-start.1 = (f32[16,16]{1,0:T(8,128)S(1)}, f32[16,16]{1,0:T(8,128)}, u32[]{:S(2)}) copy-start(f32[16,16]{1,0:T(8,128)} %param.8) | copy-start | bytes 3076
Sparse Core Ops, SparseCore 0:
  9.7 44.1 all-gather.4
  61.4 31.8 all-gather.6
  98.8 175.7 all-gather.8
  362.7 72.0 all-gather.10
where the time goes:
time: 700 us; the launch traced here: 695 us
  waiting for transfers between devices  324 us (46%)
  matrix products  307 us (44%)
  local copies, waits for them, and re-layouts  49.8 us (7%)
  between operations  13.6 us (2%)
    dot_general x4, matrix products, per_device(): jnp.einsum('wpq,wqr->wpr', screened * coulomb, coupling, precision=lax.Pr...  237 us
    all_gather x1, waiting for transfers between devices, per_device(): lax.all_gather(mixed, 'aux', axis=1, tiled=True)  176 us
    all_gather x1, waiting for transfers between devices, per_device(): lax.all_gather(chi_freq[:, ::stride, :], 'aux', axis=1, tiled=True)  72.2 us
    dot_general x1, matrix products, per_device(): jnp.einsum('pk,wkq->wpq', wide_coef, lax.all_gather(mixed, 'aux', axis=1,...  59.4 us
    all_gather x1, waiting for transfers between devices, per_device(): panel_coef = lax.all_gather(local_panel, 'aux', axis=0, tiled=True)  44.3 us
    all_gather x1, waiting for transfers between devices, per_device(): gathered = lax.all_gather(folded, 'tau', axis=0, tiled=True)  31.9 us
    slice x2, local copies, waits for them, and re-layouts, per_device(): chi_freq[:, ::stride, :]  28.6 us
    add x1, local copies, waits for them, and re-layouts, per_device(): chi_freq + jnp.einsum('wpq,wqr->wpr', screened * coulomb, coupling, preci...  16.4 us
  transfers between devices with their start and end apart: 4, of which 4 were waited for; matrix products, arithmetic and copies ran while one was open for 0% of the time, Pallas kernels for 0%

commit v1 on v0

--- a/solution.py
+++ b/solution.py
@@ -30,7 +30,7 @@
         lax.all_gather(mixed, "aux", axis=1, tiled=True),
         precision=lax.Precision.HIGHEST,
     )
-    coupling = lax.all_gather(chi_freq[:, ::stride, :], "aux", axis=1, tiled=True)
+    coupling = jnp.concatenate(lax.all_gather(chi_freq[:, ::stride, :], "aux"), axis=1)
     screened = chi_freq
     for sweep in range(DYSON):
         screened = chi_freq + jnp.einsum(

time: 700 us -> 672 us (0.960)
  matrix products: 307 us -> 267 us
  local copies, waits for them, and re-layouts: 49.8 us -> 61.4 us
    dot_general x4, matrix products: 237 us -> 197 us  [per_device(): jnp.einsum('wpq,wqr->wpr', screened * coulomb, coupling, precision=lax.Pr...]
    all_gather x0 -> x1, local copies, waits for them, and re-layouts: none -> 9.65 us  [per_device(): lax.all_gather(chi_freq[:, ::stride, :], 'aux')]
where the time goes in v1:
time: 672 us; the launch traced here: 667 us
  waiting for transfers between devices  324 us (48%)
  matrix products  267 us (40%)
  local copies, waits for them, and re-layouts  61.4 us (9%)
  between operations  13.6 us (2%)
    dot_general x4, matrix products, per_device(): jnp.einsum('wpq,wqr->wpr', screened * coulomb, coupling, precision=lax.Pr...  197 us
    all_gather x1, waiting for transfers between devices, per_device(): lax.all_gather(mixed, 'aux', axis=1, tiled=True)  176 us
    all_gather x1, waiting for transfers between devices, per_device(): lax.all_gather(chi_freq[:, ::stride, :], 'aux')  72.2 us
    dot_general x1, matrix products, per_device(): jnp.einsum('pk,wkq->wpq', wide_coef, lax.all_gather(mixed, 'aux', axis=1,...  59.4 us
    all_gather x1, waiting for transfers between devices, per_device(): panel_coef = lax.all_gather(local_panel, 'aux', axis=0, tiled=True)  44.3 us
    all_gather x1, waiting for transfers between devices, per_device(): gathered = lax.all_gather(folded, 'tau', axis=0, tiled=True)  31.9 us
    slice x2, local copies, waits for them, and re-layouts, per_device(): chi_freq[:, ::stride, :]  29 us
    add x1, local copies, waits for them, and re-layouts, per_device(): chi_freq + jnp.einsum('wpq,wqr->wpr', screened * coulomb, coupling, preci...  16.4 us
  transfers between devices with their start and end apart: 4, of which 4 were waited for; matrix products, arithmetic and copies ran while one was open for 0% of the time, Pallas kernels for 0%

profile of v1, /device:TPU:0, one launch (start us, length us, event | category | flops | bytes accessed | tf_op | source)
XLA Modules:
  0.0 666.7 jit_solution(2894668255691026430)
XLA Ops:
  6.5 0.0 copy-start
  6.5 0.0 all-gather.6.cloned.1.call-start
  6.5 3.0 slice.6
  9.5 0.0 all-gather.6.cloned.1.call-update
  9.5 0.0 all-gather.8.cloned.1.call-start
  9.6 44.3 %all-gather.6.cloned.1.call-done = bf16[512,2048]{1,0:T(8,128)(2,1)} async-done(((bf16[32,2048]{1,0:T(8,128)(2,1)}), bf16[512,2048]{1,0:T(8,128)(2,1)}) %all-gather.6.cloned.1.call-update) | async-done | bytes 2097168 | tf_op jit(solution)/shard_map/all_gather | solution.py:14
  53.9 7.4 %fusion.23 = bf16[8,128,512]{2,1,0:T(8,128)(2,1)} fusion(bf16[512,2048]{1,0:T(8,128)(2,1)} %all-gather.6.cloned.1.call-done, bf16[8,128,2048]{2,1,0:T(8,128)(2,1)} %param.7, bf16[8,128,2048]{2,1,0:T(8,128)(2,1)} %param.6), kind=kOutput, calls=%fused_computation.23 | convolution fusion | flops 2156396544 | bytes 11534336 | tf_op jit(solution)/shard_map/tkn,qn->tkq/dot_general | solution.py:16
  61.3 0.0 all-gather.8.cloned.1.call-update
  61.3 0.0 all-gather.10.cloned.1.call-start
  61.3 31.9 %all-gather.8.cloned.1.call-done = bf16[16,128,512]{2,1,0:T(8,128)(2,1)} async-done(((bf16[8,128,512]{2,1,0:T(8,128)(2,1)}), bf16[16,128,512]{2,1,0:T(8,128)(2,1)}) %all-gather.8.cloned.1.call-update) | async-done | bytes 2097168 | tf_op jit(solution)/shard_map/all_gather | solution.py:22
  93.3 0.0 copy-done
  93.3 3.5 fusion.21
  96.7 1.9 copy.16
  98.6 0.0 all-gather.10.cloned.1.call-update
  98.6 0.3 all-gather.12.cloned.1.call-start
  98.9 175.6 %all-gather.10.cloned.1.call-done = f32[8,2048,512]{1,2,0:T(8,128)} async-done(((f32[8,128,512]{1,2,0:T(8,128)}), f32[8,2048,512]{1,2,0:T(8,128)}) %all-gather.10.cloned.1.call-update) | async-done | bytes 33554448 | tf_op jit(solution)/shard_map/all_gather | solution.py:30
  274.5 59.4 %convolution_bitcast_fusion = f32[8,1024,512]{1,2,0:T(8,128)} fusion(f32[8,2048,512]{1,2,0:T(8,128)} %all-gather.10.cloned.1.call-done, bf16[1024,2048]{1,0:T(8,128)(2,1)} %param.5), kind=kOutput, calls=%fused_computation.12 | convolution fusion | flops 103079215104 | bytes 54525952 | tf_op jit(solution)/shard_map/pk,wkq->wpq/dot_general | solution.py:27
  333.9 27.5 %slice.7 = f32[8,32,512]{1,2,0:T(8,128)S(1)} slice(f32[8,1024,512]{1,2,0:T(8,128)} %convolution_bitcast_fusion), slice={[0:8:1], [0:1024:32], [0:512:1]} | slice | bytes 1048576 | tf_op jit(solution)/shard_map/slice | solution.py:33
  361.5 1.4 copy.10
  362.9 0.0 all-gather.12.cloned.1.call-update
  362.9 72.2 %all-gather.12.cloned.1.call-done = f32[128,32,512]{2,1,0:T(8,128)} async-done(((f32[8,32,512]{2,1,0:T(8,128)}), f32[128,32,512]{2,1,0:T(8,128)}) %all-gather.12.cloned.1.call-update) | async-done | bytes 8388624 | tf_op jit(solution)/shard_map/all_gather | solution.py:33
  435.2 9.7 %copy.11 = f32[16,8,32,512]{3,2,0,1:T(8,128)} copy(f32[16,8,32,512]{3,2,1,0:T(8,128)} %bitcast.28) | data formatting | bytes 16777216 | tf_op jit(solution)/shard_map/all_gather | solution.py:33
  444.8 0.0 copy-done.3
  444.8 1.5 copy-done.2
  446.3 32.8 %fusion.9 = f32[8,1024,512]{1,2,0:T(8,128)} fusion(f32[8,512,512]{2,1,0:T(8,128)} %bitcast.22, f32[8,1024,512]{1,2,0:T(8,128)S(1)} %copy-done.2, f32[512]{0:T(512)S(1)} %copy-done.3), kind=kOutput, calls=%fused_computation.9 | convolution fusion | flops 25773998080 | bytes 41945088 | tf_op jit(solution)/shard_map/wpq,wqr->wpr/dot_general | solution.py:36
  479.2 64.2 %fusion.6 = f32[8,1024,512]{1,2,0:T(8,128)} fusion(f32[8,512,512]{2,1,0:T(8,128)} %bitcast.23, f32[8,1024,512]{1,2,0:T(8,128)} %convolution_bitcast_fusion, f32[8,1024,512]{1,2,0:T(8,128)} %fusion.9, f32[512]{0:T(512)S(1)} %copy-done.3), kind=kOutput, calls=%fused_computation.6 | convolution fusion | flops 25778192384 | bytes 58722304 | tf_op jit(solution)/shard_map/wpq,wqr->wpr/dot_general | solution.py:36
  543.4 0.0 slice-done
  543.4 0.0 slice-done.1
  543.4 35.7 %fusion.3 = f32[8,1024,512]{1,2,0:T(8,128)} fusion(f32[8,512,512]{2,1,0:T(8,128)S(1)} %bitcast.27, f32[8,1024,512]{1,2,0:T(8,128)} %convolution_bitcast_fusion, f32[8,1024,512]{1,2,0:T(8,128)} %fusion.6, f32[512]{0:T(512)S(1)} %copy-done.3), kind=kOutput, calls=%fused_computation.3 | convolution fusion | flops 25778192384 | bytes 58722304 | tf_op jit(solution)/shard_map/wpq,wqr->wpr/dot_general | solution.py:36
  579.1 64.2 %fusion.11 = f32[8,1024,512]{1,2,0:T(8,128)} fusion(f32[8,1024,512]{1,2,0:T(8,128)} %convolution_bitcast_fusion, f32[8,512,512]{2,1,0:T(8,128)} %bitcast.24, f32[8,1024,512]{1,2,0:T(8,128)} %fusion.3, f32[512]{0:T(512)S(1)} %copy-done.3), kind=kOutput, calls=%fused_computation.11 | convolution fusion | flops 25782386688 | bytes 58722304 | tf_op jit(solution)/shard_map/wpq,wqr->wpr/dot_general | solution.py:36
  643.3 16.4 %copy.14 = f32[8,1024,512]{2,1,0:T(8,128)} copy(f32[8,1024,512]{1,2,0:T(8,128)} %fusion.11) | data formatting | bytes 33554432 | tf_op jit(solution)/shard_map/add | solution.py:36
  659.7 0.0 copy-done.1
  (6 shorter events, 0.0 us)
Async XLA Ops:
  6.5 86.7 %copy-start = (f32[16,16]{1,0:T(8,128)S(1)}, f32[16,16]{1,0:T(8,128)}, u32[]{:S(2)}) copy-start(f32[16,16]{1,0:T(8,128)} %param.8) | copy-start | bytes 3076
  6.5 47.3 %all-gather.6.cloned.1.call-start = ((), (), s32[]{:S(2)}) async-start(), calls=%async_computation | async-start | bytes 2228224 | tf_op jit(solution)/shard_map/all_gather | solution.py:14
  9.5 83.7 %all-gather.8.cloned.1.call-start = ((), (), s32[]{:S(2)}) async-start(), calls=%async_computation.1 | async-start | bytes 3145728 | tf_op jit(solution)/shard_map/all_gather | solution.py:22
  61.3 213.2 %all-gather.10.cloned.1.call-start = ((), (), s32[]{:S(2)}) async-start(), calls=%async_computation.2 | async-start | bytes 35651584 | tf_op jit(solution)/shard_map/all_gather | solution.py:30
  98.6 336.5 %all-gather.12.cloned.1.call-start = ((), (), s32[]{:S(2)}) async-start(), calls=%async_computation.3 | async-start | bytes 8912896 | tf_op jit(solution)/shard_map/all_gather | solution.py:33
  333.9 110.9 %copy-start.3 = (f32[512]{0:T(512)S(1)}, f32[512]{0:T(512)}, u32[]{:S(2)}) copy-start(f32[512]{0:T(512)} %param.9) | copy-start | bytes 6148
  435.2 11.2 %copy-start.2 = (f32[8,1024,512]{1,2,0:T(8,128)S(1)}, f32[8,1024,512]{1,2,0:T(8,128)}, u32[]{:S(2)}) copy-start(f32[8,1024,512]{1,2,0:T(8,128)} %convolution_bitcast_fusion) | copy-start | bytes 50331652
  446.3 97.0 %slice-start = ((s8[8388608]{0:T(1024)(128)(4,1)}), s8[4194304]{0:T(1024)(128)(4,1)S(1)}, s32[]{:S(2)}) async-start(s8[8388608]{0:T(1024)(128)(4,1)} %bitcast.25), calls=%async_computation.4 | async-start | bytes 8388608
  479.2 64.2 %slice-start.1 = ((s8[8388608]{0:T(1024)(128)(4,1)}), s8[4194304]{0:T(1024)(128)(4,1)S(1)}, s32[]{:S(2)}) async-start(s8[8388608]{0:T(1024)(128)(4,1)} %bitcast.25), calls=%async_computation.5 | async-start | bytes 8388608
  579.1 80.7 %copy-start.1 = (f32[16,16]{1,0:T(8,128)S(1)}, f32[16,16]{1,0:T(8,128)}, u32[]{:S(2)}) copy-start(f32[16,16]{1,0:T(8,128)} %param.8) | copy-start | bytes 3076
Sparse Core Ops, SparseCore 0:
  9.7 44.1 all-gather.5
  61.4 31.8 all-gather.7
  98.8 175.7 all-gather.9
  363.1 72.0 all-gather.11
